TPU v7x, 256 devices: a whole 4x4x8 slice. The times are simulated.
256 devices in a mesh: slab: 8 (over z), filt: 32 (over y, x, core).
Axes of the slice: x: 4, y: 4, z: 8, core: 2. Of those that a mesh axis runs over, the one named last changes fastest.
Arguments:
- features: bfloat16 [32, 256, 64, 128], P('slab', 'filt'), may hold values from -6 to 6
- kernel: bfloat16 [3, 3, 3, 256, 256], P(None, None, None, 'filt'), may hold values from -0.078125 to 0.078125
- bias_vector: float32 [256], replicated, may hold values from -0.6 to 0.6
Outputs:
- activated: bfloat16 [32, 256, 64, 128], P('slab', 'filt')
All inputs are finite; a program needn't handle non-finite values.
Results may differ from a plain program's by a relative error of at most 0.005.
Values may be sent and summed in bfloat16 or wider, within the bound.
A program may use at most 128 MiB of HBM per device.

v0:
```python
import jax
import jax.numpy as jnp
from jax import lax
from jax.sharding import PartitionSpec as P

slope = 0.3


def with_halo(array, sides, width):
    for axis, dim in sides:
        devices, length = (lax.axis_size(axis), array.shape[dim])
        up = [(i, (i + 1) % devices) for i in range(devices - 1)]
        down = [(j, i) for i, j in up]
        last = lax.slice_in_dim(array, length - width, length, axis=dim)
        leading = lax.slice_in_dim(array, 0, width, axis=dim)
        before = lax.ppermute(last, axis, up)
        after = lax.ppermute(leading, axis, down)
        array = jnp.concatenate([before, array, after], axis=dim)
    return array


def convolve(volume_piece, taps, y_margin, first_center, out_count):
    in_planes, in_chan, in_rows, in_cols = volume_piece.shape
    out_chan = taps.shape[3]
    out_rows = in_rows - 2 * y_margin
    totals = [
        jnp.zeros((out_chan, out_rows, in_cols), jnp.float32) for slot_index in range(out_count)
    ]
    for plane_index in range(in_planes):
        depth_list = [
            plane_index - (first_center + slot_index) + 1 for slot_index in range(out_count)
        ]
        depth_list = [entry for entry in depth_list if 0 <= entry <= 2]
        depth_low = min(depth_list)
        depth_high = max(depth_list)
        depth_count = depth_high - depth_low + 1
        flat_weight = taps[depth_low : depth_high + 1].reshape(depth_count * 9 * out_chan, in_chan)
        products = jnp.einsum(
            "tc,cyx->tyx",
            flat_weight,
            volume_piece[plane_index],
            preferred_element_type=jnp.float32,
        )
        products = products.reshape(depth_count, 3, 3, out_chan, in_rows, in_cols)
        padded_products = jnp.pad(products, ((0, 0), (0, 0), (0, 0), (0, 0), (1, 1), (1, 1)))
        for slot_index in range(out_count):
            depth_tap = plane_index - (first_center + slot_index) + 1
            if 0 <= depth_tap <= 2:
                for row_tap in range(3):
                    for col_tap in range(3):
                        row_start = y_margin + row_tap
                        totals[slot_index] = (
                            totals[slot_index]
                            + padded_products[
                                depth_tap - depth_low,
                                row_tap,
                                col_tap,
                                :,
                                row_start : row_start + out_rows,
                                col_tap : col_tap + in_cols,
                            ]
                        )
    return jnp.stack(totals)


def finish(convolved, bias_piece):
    shifted = convolved + bias_piece[None, :, None, None]
    return jnp.where(shifted > 0, shifted, slope * shifted).astype(jnp.bfloat16)


def body(features, kernel, bias_vector):
    planes = features.shape[0]
    own_count = kernel.shape[3]
    own_bias = lax.dynamic_slice_in_dim(
        bias_vector, lax.axis_index("filt") * own_count, own_count, 0
    )
    padded = with_halo(features, (("slab", 0),), 1)
    gathered = lax.all_gather(padded, "filt", axis=1, tiled=True)
    convolved = convolve(gathered, kernel, 0, 1, planes)
    return finish(convolved, own_bias)


def solution(mesh):
    placed = (P("slab", "filt", None, None), P(None, None, None, "filt", None), P())
    return jax.shard_map(
        body, mesh=mesh, in_specs=placed, out_specs=P("slab", "filt", None, None), check_vma=False
    )
```

profile of v0, /device:TPU:1, one launch (start us, length us, event | category | flops | bytes accessed | tf_op | source)
XLA Modules:
  0.0 176.3 jit_solution(7436586387113536860)
XLA Ops:
  6.5 0.0 all-gather.2.cloned.1.call-start
  6.5 1.4 copy.4
  8.0 4.4 %collective-permute-start = (bf16[1,8,64,128]{3,1,2,0:T(8,128)(2,1)S(1)}, bf16[1,8,64,128]{3,1,2,0:T(8,128)(2,1)S(1)}, u32[]{:S(2)}, u32[]{:S(2)}) collective-permute-start(bf16[1,8,64,128]{3,1,2,0:T(8,128)(2,1)S(1)} %get-tuple-element.8), channel_id=1, source_target_pairs={{0,32},{32,64},{64,96},{96,128},{128,160},{160,192},{192,224},{1,3... | collective-permute-start | bytes 393224 | tf_op jit(solution)/shard_map/ppermute | solution.py:16
  12.3 1.3 collective-permute-start.1
  13.6 0.8 collective-permute-done
  14.5 4.2 %collective-permute-done.1 = bf16[1,8,64,128]{3,1,2,0:T(8,128)(2,1)S(1)} collective-permute-done((bf16[1,8,64,128]{3,1,2,0:T(8,128)(2,1)S(1)}, bf16[1,8,64,128]{3,1,2,0:T(8,128)(2,1)S(1)}, u32[]{:S(2)}, u32[]{:S(2)}) %collective-permute-start.1) | collective-permute-done | bytes 131104 | tf_op jit(solution)/shard_map/ppermute | solution.py:17
  18.7 1.1 pad_maximum_fusion
  19.7 0.0 all-gather.2.cloned.1.call-update
  19.7 0.8 dynamic_slice.3
  20.5 0.8 fusion.148
  21.3 1.0 fusion.149
  22.3 109.8 %all-gather.2.cloned.1.call-done = bf16[6,256,64,128]{3,1,2,0:T(8,128)(2,1)} async-done(((bf16[6,8,64,128]{3,1,2,0:T(8,128)(2,1)}), bf16[6,256,64,128]{3,1,2,0:T(8,128)(2,1)}) %all-gather.2.cloned.1.call-update) | async-done | bytes 25165840 | tf_op jit(solution)/shard_map/all_gather | solution.py:78
  132.1 3.0 %fusion = f32[64,128,72]{1,2,0:T(8,128)S(1)} fusion(bf16[72,256,1]{1,0,2:T(8,128)(2,1)S(1)} %bitcast.394, bf16[6,256,64,128]{3,1,2,0:T(8,128)(2,1)} %all-gather.2.cloned.1.call-done), kind=kOutput, calls=%fused_computation.97 | convolution fusion | flops 301989888 | bytes 6590464 | tf_op jit(solution)/shard_map/tc,cyx->tyx/dot_general | solution.py:38
  135.1 0.4 copy.23
  135.5 3.0 %fusion.5 = f32[64,128,72]{1,2,0:T(8,128)S(1)} fusion(bf16[72,256,1]{1,0,2:T(8,128)(2,1)S(1)} %bitcast.393, bf16[6,256,64,128]{3,1,2,0:T(8,128)(2,1)} %all-gather.2.cloned.1.call-done), kind=kOutput, calls=%fused_computation.107 | convolution fusion | flops 301989888 | bytes 6590464 | tf_op jit(solution)/shard_map/tc,cyx->tyx/dot_general | solution.py:38
  138.6 1.8 %copy.7 = f32[1,3,3,8,64,128]{5,4,3,2,1,0:T(8,128)} copy(f32[1,3,3,8,64,128]{5,3,2,1,4,0:T(8,128)S(1)} %bitcast.388) | data formatting | bytes 4718592 | tf_op jit(solution)/shard_map/reshape | solution.py:44
  140.4 3.0 %fusion.1 = f32[64,128,144]{1,2,0:T(8,128)S(1)} fusion(bf16[144,256,1]{1,0,2:T(8,128)(2,1)S(1)} %bitcast.392, bf16[6,256,64,128]{3,1,2,0:T(8,128)(2,1)} %all-gather.2.cloned.1.call-done), kind=kOutput, calls=%fused_computation.99 | convolution fusion | flops 603979776 | bytes 8986624 | tf_op jit(solution)/shard_map/tc,cyx->tyx/dot_general | solution.py:38
  143.4 3.6 %copy.19 = f32[2,3,3,8,64,128]{5,4,3,2,1,0:T(8,128)} copy(f32[2,3,3,8,64,128]{5,3,2,1,0,4:T(8,128)S(1)} %bitcast.385) | data formatting | bytes 9437184 | tf_op jit(solution)/shard_map/reshape | solution.py:44
  147.0 0.0 copy-start
  147.0 3.0 %fusion.4 = f32[64,128,144]{1,2,0:T(8,128)S(1)} fusion(bf16[144,256,1]{1,0,2:T(8,128)(2,1)S(1)} %bitcast.391, bf16[6,256,64,128]{3,1,2,0:T(8,128)(2,1)} %all-gather.2.cloned.1.call-done), kind=kOutput, calls=%fused_computation.105 | convolution fusion | flops 603979776 | bytes 8986624 | tf_op jit(solution)/shard_map/tc,cyx->tyx/dot_general | solution.py:38
  150.0 1.4 copy.9
  151.4 0.0 copy-done
  151.4 3.3 %fusion.3 = f32[64,128,216]{1,2,0:T(8,128)S(1)} fusion(bf16[216,256,1]{1,0,2:T(8,128)(2,1)S(1)} %bitcast.389, bf16[6,256,64,128]{3,1,2,0:T(8,128)(2,1)} %all-gather.2.cloned.1.call-done), kind=kOutput, calls=%fused_computation.103 | convolution fusion | flops 905969664 | bytes 11382784 | tf_op jit(solution)/shard_map/tc,cyx->tyx/dot_general | solution.py:38
  154.7 1.3 copy.11
  156.0 3.3 %fusion.2 = f32[64,128,216]{1,2,0:T(8,128)S(1)} fusion(bf16[216,256,1]{1,0,2:T(8,128)(2,1)S(1)} %bitcast.390, bf16[6,256,64,128]{3,1,2,0:T(8,128)(2,1)} %all-gather.2.cloned.1.call-done), kind=kOutput, calls=%fused_computation.101 | convolution fusion | flops 905969664 | bytes 11382784 | tf_op jit(solution)/shard_map/tc,cyx->tyx/dot_general | solution.py:38
  159.3 0.0 slice-start
  159.3 1.3 copy.15
  160.7 0.0 slice-start.1
  160.7 3.3 %fusion.123 = f32[1,8,64,128]{3,2,1,0:T(8,128)S(1)} fusion(f32[3,3,3,8,64,128]{5,4,3,2,1,0:T(8,128)S(1)} %copy.11, f32[2,3,3,8,64,128]{5,4,3,2,1,0:T(8,128)S(1)} %copy.9, f32[1,3,3,8,64,128]{5,4,3,2,1,0:T(8,128)} %copy.7), kind=kLoop, calls=%fused_computation.228 | loop fusion | flops 1703936 | bytes 15204352 | tf_op jit(solution)/shard_map/add | solution.py:53
  164.0 0.0 slice-done
  164.0 0.0 slice-done.1
  164.0 4.4 %fusion.142 = (f32[1,8,64,128]{3,2,1,0:T(8,128)S(1)}, f32[1,8,64,128]{3,2,1,0:T(8,128)S(1)}, f32[1,8,64,128]{3,2,1,0:T(8,128)S(1)}) fusion(f32[3,3,3,8,64,128]{5,4,3,2,1,0:T(8,128)S(1)} %copy.15, f32[3,3,3,8,64,128]{5,4,3,2,1,0:T(8,128)S(1)} %copy.11, f32[2,3,3,8,64,128]{5,4,3,2,1,0:T(8,128)S(1)} %copy.9, f32[2,3,3,8,64,128]{5,4,3,2,1,0:T(8,128)S(1)} %bitcast.384, ...), kind=kLoop, calls=%fused_computation.247 | loop fusion | flops 5111808 | bytes 29097984 | tf_op jit(solution)/shard_map/add | solution.py:53
  168.4 1.0 fusion.6
  (2 shorter events, 0.0 us)
Async XLA Ops:
  6.5 125.6 %all-gather.2.cloned.1.call-start = ((), (), s32[]{:S(2)}) async-start(), calls=%async_computation | async-start | bytes 25952256 | tf_op jit(solution)/shard_map/all_gather | solution.py:78
  8.0 6.5 %collective-permute-start = (bf16[1,8,64,128]{3,1,2,0:T(8,128)(2,1)S(1)}, bf16[1,8,64,128]{3,1,2,0:T(8,128)(2,1)S(1)}, u32[]{:S(2)}, u32[]{:S(2)}) collective-permute-start(bf16[1,8,64,128]{3,1,2,0:T(8,128)(2,1)S(1)} %get-tuple-element.8), channel_id=1, source_target_pairs={{0,32},{32,64},{64,96},{96,128},{128,160},{160,192},{192,224},{1,3... | collective-permute-start | bytes 393224 | tf_op jit(solution)/shard_map/ppermute | solution.py:16
  12.3 6.3 %collective-permute-start.1 = (bf16[1,8,64,128]{3,1,2,0:T(8,128)(2,1)S(1)}, bf16[1,8,64,128]{3,1,2,0:T(8,128)(2,1)S(1)}, u32[]{:S(2)}, u32[]{:S(2)}) collective-permute-start(bf16[1,8,64,128]{3,1,2,0:T(8,128)(2,1)S(1)} %get-tuple-element.9), channel_id=1, source_target_pairs={{32,0},{64,32},{96,64},{128,96},{160,128},{192,160},{224,192},{33,... | collective-permute-start | bytes 393224 | tf_op jit(solution)/shard_map/ppermute | solution.py:17
  147.0 4.4 %copy-start = (bf16[3,3,3,8,256]{4,3,2,1,0:T(8,128)(2,1)S(1)}, bf16[3,3,3,8,256]{4,3,2,1,0:T(8,128)(2,1)}, u32[]{:S(2)}) copy-start(bf16[3,3,3,8,256]{4,3,2,1,0:T(8,128)(2,1)} %param.4) | copy-start | bytes 331780
  159.3 4.7 %slice-start = ((s8[4718592]{0:T(1024)(128)(4,1)}), s8[524288]{0:T(1024)(128)(4,1)S(1)}, s32[]{:S(2)}) async-start(s8[4718592]{0:T(1024)(128)(4,1)} %bitcast.383), calls=%async_computation.1 | async-start | bytes 1048576
  160.7 3.3 %slice-start.1 = ((s8[4718592]{0:T(1024)(128)(4,1)}), s8[4194304]{0:T(1024)(128)(4,1)S(1)}, s32[]{:S(2)}) async-start(s8[4718592]{0:T(1024)(128)(4,1)} %bitcast.383), calls=%async_computation.2 | async-start | bytes 8388608
Sparse Core Ops, SparseCore 0:
  19.9 112.1 all-gather.1
where the time goes:
time: 177 us; the launch traced here: 176 us
  waiting for transfers between devices  115 us (65%)
  matrix products  18.6 us (11%)
  local copies, waits for them, and re-layouts  13.8 us (8%)
  between operations  13.6 us (8%)
  other arithmetic  9.79 us (6%)
  starting transfers between devices  5.67 us (3%)
    all_gather x1, waiting for transfers between devices, body(): gathered = lax.all_gather(padded, 'filt', axis=1, tiled=True)  110 us
    dot_general x6, matrix products, convolve(): jnp.einsum('tc,cyx->tyx', flat_weight, volume_piece[plane_index], preferr...  18.6 us
    reshape x6, local copies, waits for them, and re-layouts, convolve(): products = products.reshape(depth_count, 3, 3, out_chan, in_rows, in_cols)  9.91 us
    add x2, other arithmetic, convolve(): totals[slot_index]  7.69 us
    ppermute x1, starting transfers between devices, with_halo(): before = lax.ppermute(last, axis, up)  4.38 us
    ppermute x1, waiting for transfers between devices, with_halo(): after = lax.ppermute(leading, axis, down)  4.18 us
  transfers between devices with their start and end apart: 3, of which 3 were waited for; matrix products, arithmetic and copies ran while one was open for 1% of the time, Pallas kernels for 0%

commit v1 on v0

--- a/solution.py
+++ b/solution.py
@@ -75,7 +75,9 @@
         bias_vector, lax.axis_index("filt") * own_count, own_count, 0
     )
     padded = with_halo(features, (("slab", 0),), 1)
-    gathered = lax.all_gather(padded, "filt", axis=1, tiled=True)
+    gathered = jnp.concatenate(
+        lax.all_to_all(jnp.stack([padded] * lax.axis_size("filt")), "filt", 0, 0), axis=1
+    )
     convolved = convolve(gathered, kernel, 0, 1, planes)
     return finish(convolved, own_bias)
 

time: 177 us -> 398 us (2.25)
  the two profiles are of different devices: /device:TPU:1 before, /device:TPU:96 now
where the time goes in v1:
time: 398 us
  waiting for transfers between devices  328 us (82%)
  local copies, waits for them, and re-layouts  37.6 us (9%)
  starting transfers between devices  14.5 us (4%)
  matrix products  9.81 us (2%)
  other arithmetic  8.14 us (2%)
    all_to_all x1, waiting for transfers between devices, body(): lax.all_to_all(jnp.stack([padded] * lax.axis_size('filt')), 'filt', 0, 0)  321 us
    slice x1, local copies, waits for them, and re-layouts, convolve(): volume_piece[plane_index]  17.2 us
    dot_general x6, matrix products, convolve(): jnp.einsum('tc,cyx->tyx', flat_weight, volume_piece[plane_index], preferr...  9.81 us
    another operation x1, local copies, waits for them, and re-layouts, body(): jnp.stack([padded] * lax.axis_size('filt'))  9.12 us
  transfers between devices with their start and end apart: 3, of which 3 were waited for; matrix products, arithmetic and copies ran while one was open for 0% of the time, Pallas kernels for 0%

profile of v1, /device:TPU:96, one launch (start us, length us, event | category | flops | bytes accessed | tf_op | source)
XLA Modules:
  0.0 397.7 jit_solution(12823796032234253907)
XLA Ops:
  0.0 1.0 fusion.160
  1.0 5.0 %collective-permute-start = (bf16[1,8,64,128]{3,2,1,0:T(8,128)(2,1)S(1)}, bf16[1,8,64,128]{3,2,1,0:T(8,128)(2,1)S(1)}, u32[]{:S(2)}, u32[]{:S(2)}) collective-permute-start(bf16[1,8,64,128]{3,2,1,0:T(8,128)(2,1)S(1)} %get-tuple-element.14), channel_id=1, source_target_pairs={{0,32},{32,64},{64,96},{96,128},{128,160},{160,192},{192,224},{1,3... | collective-permute-start | bytes 393224 | tf_op jit(solution)/shard_map/ppermute | solution.py:16
  6.0 1.9 collective-permute-start.1
  8.0 0.8 collective-permute-done
  8.8 5.3 %collective-permute-done.1 = bf16[1,8,64,128]{3,2,1,0:T(8,128)(2,1)S(1)} collective-permute-done((bf16[1,8,64,128]{3,2,1,0:T(8,128)(2,1)S(1)}, bf16[1,8,64,128]{3,2,1,0:T(8,128)(2,1)S(1)}, u32[]{:S(2)}, u32[]{:S(2)}) %collective-permute-start.1) | collective-permute-done | bytes 131104 | tf_op jit(solution)/shard_map/ppermute | solution.py:17
  14.1 1.1 pad_maximum_fusion
  15.2 0.5 copy.23
  15.8 9.1 %stack.4 = bf16[32,6,8,64,128]{4,2,3,1,0:T(8,128)(2,1)} broadcast(bf16[6,8,64,128]{3,1,2,0:T(8,128)(2,1)S(1)} %copy.23), dimensions={1,2,3,4} | broadcast | bytes 25952256 | tf_op jit(solution)/shard_map/stack | solution.py:79
  24.9 0.0 copy-start.5
  24.9 0.0 copy-start.4
  24.9 7.6 %all-to-all-start = ((bf16[32,6,8,64,128]{4,2,3,1,0:T(8,128)(2,1)}), bf16[32,6,8,64,128]{4,2,3,1,0:T(8,128)(2,1)}, u32[]{:S(2)}, u32[]{:S(2)}) async-start(bf16[32,6,8,64,128]{4,2,3,1,0:T(8,128)(2,1)} %stack.4), calls=%async_computation | async-start | bytes 50331648 | tf_op jit(solution)/shard_map/all_to_all | solution.py:79
  32.5 0.0 copy-done.5
  32.5 0.1 dynamic_slice.3
  32.6 0.0 copy-done.4
  32.6 321.4 %all-to-all-done = bf16[32,6,8,64,128]{4,2,3,1,0:T(8,128)(2,1)} async-done(((bf16[32,6,8,64,128]{4,2,3,1,0:T(8,128)(2,1)}), bf16[32,6,8,64,128]{4,2,3,1,0:T(8,128)(2,1)}, u32[]{:S(2)}, u32[]{:S(2)}) %all-to-all-start) | async-done | bytes 25165856 | tf_op jit(solution)/shard_map/all_to_all | solution.py:79
  354.0 17.2 %fusion.159 = (bf16[1,32,8,64,128]{4,2,3,0,1:T(8,128)(2,1)}, bf16[1,32,8,64,128]{4,2,3,0,1:T(8,128)(2,1)}, bf16[1,32,8,64,128]{4,2,3,0,1:T(8,128)(2,1)}, bf16[1,...) fusion(bf16[6,32,8,64,128]{4,2,3,0,1:T(8,128)(2,1)} %bitcast), kind=kLoop, calls=%fused_computation.262 | loop fusion | bytes 50331648 | tf_op jit(solution)/shard_map/slice | solution.py:41
  371.2 3.3 fusion.6
  374.5 0.0 copy-start.1
  374.5 1.3 copy.31
  375.9 0.8 copy-done.1
  376.7 0.8 fusion.8
  377.5 0.0 copy-start
  377.5 1.4 copy.28
  378.9 0.8 copy-done
  379.7 1.1 fusion.4
  380.8 1.3 copy.36
  382.1 3.0 fusion.2
  385.1 0.0 copy-start.3
  385.1 1.4 copy.41
  386.5 0.8 copy-done.3
  387.3 0.0 copy-start.2
  387.3 0.8 fusion
  388.1 0.4 copy.46
  388.6 0.9 copy-done.2
  389.5 0.8 fusion.10
  390.3 0.4 copy.25
  390.7 1.6 fusion.135
  392.4 4.3 %fusion.154 = (f32[1,8,64,128]{3,2,1,0:T(8,128)S(1)}, f32[1,8,64,128]{3,2,1,0:T(8,128)S(1)}, f32[1,8,64,128]{3,2,1,0:T(8,128)S(1)}) fusion(f32[3,3,3,8,64,128]{5,4,3,2,1,0:T(8,128)S(1)} %copy.36, f32[3,3,3,8,64,128]{5,4,3,2,1,0:T(8,128)S(1)} %copy.31, f32[2,3,3,8,64,128]{5,4,3,2,1,0:T(8,128)S(1)} %copy.28, f32[2,3,3,8,64,128]{5,4,3,2,1,0:T(8,128)S(1)} %copy.41, ...), kind=kLoop, calls=%fused_computation.253 | loop fusion | flops 5111808 | bytes 29097984 | tf_op jit(solution)/shard_map/add | solution.py:53
  396.7 1.0 fusion.18
  (2 shorter events, 0.0 us)
Async XLA Ops:
  1.0 7.8 %collective-permute-start = (bf16[1,8,64,128]{3,2,1,0:T(8,128)(2,1)S(1)}, bf16[1,8,64,128]{3,2,1,0:T(8,128)(2,1)S(1)}, u32[]{:S(2)}, u32[]{:S(2)}) collective-permute-start(bf16[1,8,64,128]{3,2,1,0:T(8,128)(2,1)S(1)} %get-tuple-element.14), channel_id=1, source_target_pairs={{0,32},{32,64},{64,96},{96,128},{128,160},{160,192},{192,224},{1,3... | collective-permute-start | bytes 393224 | tf_op jit(solution)/shard_map/ppermute | solution.py:16
  6.0 8.1 %collective-permute-start.1 = (bf16[1,8,64,128]{3,2,1,0:T(8,128)(2,1)S(1)}, bf16[1,8,64,128]{3,2,1,0:T(8,128)(2,1)S(1)}, u32[]{:S(2)}, u32[]{:S(2)}) collective-permute-start(bf16[1,8,64,128]{3,2,1,0:T(8,128)(2,1)S(1)} %get-tuple-element.15), channel_id=1, source_target_pairs={{32,0},{64,32},{96,64},{128,96},{160,128},{192,160},{224,192},{33,... | collective-permute-start | bytes 393224 | tf_op jit(solution)/shard_map/ppermute | solution.py:17
  24.9 7.6 %copy-start.5 = (f32[256]{0:T(256)S(1)}, f32[256]{0:T(256)}, u32[]{:S(2)}) copy-start(f32[256]{0:T(256)} %param.5) | copy-start | bytes 3076
  24.9 7.7 %copy-start.4 = (bf16[3,3,3,8,256]{4,3,2,1,0:T(8,128)(2,1)S(1)}, bf16[3,3,3,8,256]{4,3,2,1,0:T(8,128)(2,1)}, u32[]{:S(2)}) copy-start(bf16[3,3,3,8,256]{4,3,2,1,0:T(8,128)(2,1)} %param.4) | copy-start | bytes 331780
  24.9 329.1 %all-to-all-start = ((bf16[32,6,8,64,128]{4,2,3,1,0:T(8,128)(2,1)}), bf16[32,6,8,64,128]{4,2,3,1,0:T(8,128)(2,1)}, u32[]{:S(2)}, u32[]{:S(2)}) async-start(bf16[32,6,8,64,128]{4,2,3,1,0:T(8,128)(2,1)} %stack.4), calls=%async_computation | async-start | bytes 50331648 | tf_op jit(solution)/shard_map/all_to_all | solution.py:79
  374.5 2.2 copy-start.1
  377.5 2.2 copy-start
  385.1 2.2 copy-start.3
  387.3 2.2 copy-start.2
